TPU v7x, 32 devices: a whole 2x2x4 slice. The times are simulated.
32 devices in a mesh: seq: 4 (over x, core), head: 8 (over z, y).
Axes of the slice: x: 2, y: 2, z: 4, core: 2. Of those that a mesh axis runs over, the one named last changes fastest.
Arguments:
- inner_input: bfloat16 [2048, 16384], P('seq', 'head'), may hold values from -6 to 6
- gate_input: bfloat16 [2048, 16384], P('seq', 'head'), may hold values from -48 to 48
- bc_input: bfloat16 [2048, 4096], P('seq'), may hold values from -6 to 6
- dt_input: float32 [256, 2048], P('head', 'seq'), may hold values from -11.5 to 0
- log_rate: float32 [256], P('head'), may hold values from -1.2 to 0
- skip_weight: float32 [256], P('head'), may hold values from 0.5 to 1.5
- conv_weight_x: float32 [4, 16384], P(None, 'head'), may hold values from -3 to 3
- conv_bias_x: float32 [16384], P('head'), may hold values from -3 to 3
- conv_weight_bc: float32 [4, 4096], replicated, may hold values from -3 to 3
- conv_bias_bc: float32 [4096], replicated, may hold values from -3 to 3
- conv_tail_x: bfloat16 [3, 16384], P(None, 'head'), may hold values from -6 to 6
- conv_tail_bc: bfloat16 [3, 4096], replicated, may hold values from -6 to 6
- init_state: float32 [256, 64, 256], P('head'), may hold values from -0.6 to 0.6
- norm_gain: float32 [16384], P('head'), may hold values from 0.5 to 1.5
- out_weight: bfloat16 [16384, 8192], P('head', 'seq'), may hold values from -0.046875 to 0.046875
Outputs:
- layer_out: bfloat16 [2048, 8192], P(('seq', 'head'))
- boundary_states: float32 [4, 256, 64, 256], P('seq', 'head')
All inputs are finite; a program needn't handle non-finite values.
Results may differ from a plain program's by a relative error of at most 0.015.
Values may be sent and summed in bfloat16 or wider, within the bound.
A program may use at most 192 MiB of HBM per device.

v0:
```python
import jax
import jax.numpy as jnp
from jax import lax
from jax.sharding import PartitionSpec as P

MIXER_HEADS = 256
HEADDIM = 64
STATE = 256
GROUPS = 8
KERNEL = 4
SPAN = 128
DINNER = 16384
highest = lax.Precision.HIGHEST
norm_eps = 1e-05


def from_behind(x, axis, by):
    count = lax.axis_size(axis)
    pairs = [(i, i + by) for i in range(count) if 0 <= i + by < count]
    return lax.ppermute(x, axis, pairs)


def carried_in(x, axis, join, neutral):
    place = lax.axis_index(axis)
    gathered = jax.tree.map(
        lambda a, kind: lax.all_gather(a.astype(kind), axis), x, (jnp.bfloat16, jnp.bfloat16)
    )
    state = jax.tree.map(lambda a, e: jnp.zeros_like(a) + jnp.asarray(e, a.dtype), x, neutral)

    def one(lap, state):
        return join(
            state,
            jax.tree.map(
                lambda a, own: lax.dynamic_index_in_dim(a, lap, 0, False).astype(own.dtype),
                gathered,
                x,
            ),
        )

    return lax.fori_loop(0, place, one, state)


def causal_conv(values, previous, kernel_weight, kernel_bias):
    extended = jnp.concatenate([previous, values], axis=0)
    length = values.shape[0]
    running = jnp.zeros_like(values) + kernel_bias[None, :]
    for offset in range(KERNEL):
        running = running + kernel_weight[offset][None, :] * extended[offset : offset + length]
    return running


def ssd_block(span_x, span_b, span_c, span_step, span_log, state):
    cumul = jnp.cumsum(span_log, axis=1)
    length = span_x.shape[0]
    causal = (jnp.arange(length)[:, None] >= jnp.arange(length)[None, :])[None]
    spread = jnp.where(causal, cumul[:, :, None] - cumul[:, None, :], 0.0)
    decays = jnp.where(causal, jnp.exp(spread), 0.0)
    scores = jnp.einsum("thn,shn->hts", span_c, span_b, precision=highest)
    mixer = scores * decays * span_step[:, None, :]
    output = jnp.einsum("hts,shp->thp", mixer, span_x, precision=highest)
    carried = jnp.einsum("thn,hpn->thp", span_c, state, precision=highest)
    output = output + jnp.exp(cumul).T[:, :, None] * carried
    weights = jnp.exp(cumul[:, -1:] - cumul) * span_step
    written = jnp.einsum("hs,shp,shn->hpn", weights, span_x, span_b, precision=highest)
    new_state = jnp.exp(cumul[:, -1])[:, None, None] * state + written
    return (output, new_state)


def body(
    inner_input,
    gate_input,
    bc_input,
    dt_input,
    log_rate,
    skip_weight,
    conv_weight_x,
    conv_bias_x,
    conv_weight_bc,
    conv_bias_bc,
    conv_tail_x,
    conv_tail_bc,
    init_state,
    norm_gain,
    out_weight,
):
    seq_index = lax.axis_index("seq")
    head_index = lax.axis_index("head")
    row_count = inner_input.shape[0]
    channels = inner_input.shape[1]
    heads_here = dt_input.shape[0]
    per_group = MIXER_HEADS // GROUPS
    heads_shared = min(heads_here, per_group)
    groups_here = heads_here // heads_shared
    group_first = head_index * heads_here // per_group
    width_bc = groups_here * STATE

    def own_columns(table, table_dim):
        part_b = lax.dynamic_slice_in_dim(table, group_first * STATE, width_bc, table_dim)
        part_c = lax.dynamic_slice_in_dim(
            table, GROUPS * STATE + group_first * STATE, width_bc, table_dim
        )
        return jnp.concatenate([part_b, part_c], axis=table_dim)

    own_bc = own_columns(bc_input, 1)
    tail_rows = row_count - KERNEL + 1
    arrived = from_behind((inner_input[tail_rows:], own_bc[tail_rows:]), "seq", 1)
    at_first = seq_index == 0
    previous_x = jnp.where(at_first, conv_tail_x, arrived[0])
    previous_bc = jnp.where(at_first, own_columns(conv_tail_bc, 1), arrived[1])
    conv_x = jax.nn.silu(
        causal_conv(
            inner_input.astype(jnp.float32),
            previous_x.astype(jnp.float32),
            conv_weight_x,
            conv_bias_x,
        )
    ).astype(jnp.bfloat16)
    conv_bc = jax.nn.silu(
        causal_conv(
            own_bc.astype(jnp.float32),
            previous_bc.astype(jnp.float32),
            own_columns(conv_weight_bc, 1),
            own_columns(conv_bias_bc, 0),
        )
    ).astype(jnp.bfloat16)
    stride_length = jax.nn.softplus(dt_input)
    decay_log = -jnp.exp(log_rate)[:, None] * stride_length
    spans_here = row_count // SPAN
    all_x = conv_x.astype(jnp.float32).reshape(row_count, heads_here, HEADDIM)
    bc_float = conv_bc.astype(jnp.float32)
    all_b = jnp.repeat(
        bc_float[:, :width_bc].reshape(row_count, groups_here, STATE), heads_shared, axis=1
    )
    all_c = jnp.repeat(
        bc_float[:, width_bc:].reshape(row_count, groups_here, STATE), heads_shared, axis=1
    )

    def span_step_body(state, span_index):
        first_row = span_index * SPAN
        span_x = lax.dynamic_slice_in_dim(all_x, first_row, SPAN, 0)
        span_b = lax.dynamic_slice_in_dim(all_b, first_row, SPAN, 0)
        span_c = lax.dynamic_slice_in_dim(all_c, first_row, SPAN, 0)
        span_step = lax.dynamic_slice_in_dim(stride_length, first_row, SPAN, 1)
        span_log = lax.dynamic_slice_in_dim(decay_log, first_row, SPAN, 1)
        output, new_state = ssd_block(span_x, span_b, span_c, span_step, span_log, state)
        return (new_state, output)

    empty_state = jnp.zeros((heads_here, HEADDIM, STATE), jnp.float32)
    local_state, local_out = lax.scan(
        span_step_body, empty_state, jnp.arange(spans_here, dtype=jnp.int32)
    )
    local_out = local_out.reshape(row_count, heads_here, HEADDIM)
    cumul = jnp.cumsum(decay_log, axis=1)
    total_log = cumul[:, -1]

    def combine(earlier, later):
        return (earlier[0] + later[0], jnp.exp(later[0])[:, None, None] * earlier[1] + later[1])

    identity = (jnp.zeros((heads_here,), jnp.float32), empty_state)
    prior_log, prior_state = carried_in((total_log, local_state), "seq", combine, identity)
    incoming = jnp.exp(prior_log)[:, None, None] * init_state + prior_state
    incoming_term = jnp.einsum("thn,hpn->thp", all_c, incoming, precision=highest)
    outputs = (
        local_out
        + jnp.exp(cumul).T[:, :, None] * incoming_term
        + skip_weight[None, :, None] * all_x
    )
    boundary = (jnp.exp(total_log)[:, None, None] * incoming + local_state)[None]
    mixed = outputs.reshape(row_count, channels) * jax.nn.silu(gate_input.astype(jnp.float32))
    group_width = DINNER // GROUPS
    piece_width = min(channels, group_width)
    pieces_here = channels // piece_width
    pieces = mixed.reshape(row_count, pieces_here, piece_width)
    squares = jnp.sum(pieces * pieces, axis=2).T
    own_group = (head_index * pieces_here + jnp.arange(pieces_here)) * piece_width // group_width
    membership = (own_group[:, None] == jnp.arange(GROUPS)[None, :]).astype(jnp.float32)
    contribution = jnp.dot(membership.T, squares, precision=highest)
    group_totals = lax.psum(contribution, "head")
    group_sums = jnp.dot(membership, group_totals, precision=highest)
    inverse_rms = lax.rsqrt(group_sums / group_width + norm_eps).T
    normed = (
        (pieces * inverse_rms[:, :, None]).reshape(row_count, channels) * norm_gain[None, :]
    ).astype(jnp.bfloat16)
    terms = jnp.dot(
        normed,
        lax.all_gather(out_weight, "seq", axis=1, tiled=True),
        preferred_element_type=jnp.float32,
    )
    layer_out = lax.psum_scatter(
        terms.astype(jnp.bfloat16), "head", scatter_dimension=0, tiled=True
    )
    return (layer_out, boundary)


def solution(mesh):
    in_specs = (
        P("seq", "head"),
        P("seq", "head"),
        P("seq", None),
        P("head", "seq"),
        P("head"),
        P("head"),
        P(None, "head"),
        P("head"),
        P(),
        P(),
        P(None, "head"),
        P(),
        P("head", None, None),
        P("head"),
        P("head", "seq"),
    )
    out_specs = (P(("seq", "head"), None), P("seq", "head", None, None))
    return jax.shard_map(body, mesh=mesh, in_specs=in_specs, out_specs=out_specs, check_vma=False)
```

profile of v0, /device:TPU:0, one launch (start us, length us, event | category | flops | bytes accessed | tf_op | source)
XLA Modules:
  0.0 697.1 jit_solution(13256864626759303394)
XLA Ops:
  7.2 1.2 constant_dynamic-slice_fusion.4
  8.5 2.4 collective-permute-start.1
  11.6 4.5 collective-permute-start
  17.7 0.8 fusion.99
  18.5 0.9 fusion.98
  20.1 0.9 compare_select_fusion
  21.0 2.5 convert_element_type.65
  24.3 1.5 copy-done
  25.9 4.0 fusion.73
  29.9 5.4 copy.32
  35.2 7.6 %reshape.131 = f32[512,32,256]{2,0,1:T(8,128)} broadcast(f32[512,256]{1,0:T(8,128)S(1)} %get-tuple-element.156), dimensions={0,2} | broadcast | bytes 17301504 | tf_op jit(solution)/shard_map/reshape | solution.py:131
  42.9 7.6 %reshape.132 = f32[512,32,256]{2,0,1:T(8,128)} broadcast(f32[512,256]{1,0:T(8,128)S(1)} %get-tuple-element.155), dimensions={0,2} | broadcast | bytes 17301504 | tf_op jit(solution)/shard_map/reshape | solution.py:134
  50.5 222.8 %while.26 = (s32[]{:T(128)}, f32[32,64,256]{2,1,0:T(8,128)S(1)}, f32[4,128,32,64]{1,0,3,2:T(4,128)}, s32[4]{0:T(128)S(1)}, f32[32,512]{1,0:T(8,128)S(1)}, /*inde...) while((s32[]{:T(128)}, f32[32,64,256]{2,1,0:T(8,128)S(1)}, ...), condition=%wide.region_2.3_spmd.clone, body=%wide.region_0.2_spmd.clone.sunk | while | flops 3629928448 | bytes 34868704 | solution.py:149
  52.3 7.9 %fusion.122 = f32[32,128,128]{2,1,0:T(8,128)S(1)} fusion(f32[512,32,256]{2,0,1:T(8,128)} %get-tuple-element.312, s32[]{:T(128)S(6)} %select_n.102, f32[512,32,256]{2,0,1:T(8,128)} %get-tuple-element.311), kind=kOutput, calls=%fused_computation.6.clone.1 | convolution fusion | flops 1610612736 | bytes 10486784 | tf_op jit(solution)/shard_map/while/body/eval_jaxpr/thn,shn->hts/dot_general | solution.py:58
  60.2 6.5 fusion.123
  66.7 7.3 %fusion.124 = f32[128,32,64]{0,2,1:T(8,128)S(1)} fusion(f32[128,32,64]{0,2,1:T(8,128)} %fusion.123, f32[32,64,256]{2,1,0:T(8,128)S(1)} %get-tuple-element.291, f32[512,32,256]{2,0,1:T(8,128)} %get-tuple-element.312, s32[]{:T(128)S(6)} %select_n.102, pred[]{:T(512)S(6)} %compare.7, f32[128,32]{0,1:T(8,128)S(1)} %get-tuple-element.275), kind=kOutput, calls=%fused_computation.23.clone.1 | convolution fusion | flops 806354944 | bytes 8404997 | tf_op jit(solution)/shard_map/while/body/eval_jaxpr/thn,hpn->thp/dot_general | solution.py:61
  74.0 26.4 %dynamic_update_slice.6 = f32[4,128,32,64]{1,0,3,2:T(4,128)} dynamic-update-slice(f32[4,128,32,64]{1,0,3,2:T(4,128)} %get-tuple-element.292, f32[1,128,32,64]{1,0,3,2:T(1,128)S(1)} %bitcast.82, s32[]{:T(128)} %get-tuple-element.290, s32[]{:T(128)} %constant.87.clone.1..sunk.1, s32[]{:T(128)} %constant.87.clone.1..sunk.1, s32[]{:T(128)} %constant.87.clone.1..sunk.1) | dynamic-update-slice | bytes 2097156 | tf_op jit(solution)/shard_map/while/body/jit(dynamic_update_index_in_dim)/dynamic_update_slice | solution.py:149
  100.4 5.7 multiply_add_fusion.4
  107.9 7.9 %fusion.122 = f32[32,128,128]{2,1,0:T(8,128)S(1)} fusion(f32[512,32,256]{2,0,1:T(8,128)} %get-tuple-element.312, s32[]{:T(128)S(6)} %select_n.102, f32[512,32,256]{2,0,1:T(8,128)} %get-tuple-element.311), kind=kOutput, calls=%fused_computation.6.clone.1 | convolution fusion | flops 1610612736 | bytes 10486784 | tf_op jit(solution)/shard_map/while/body/eval_jaxpr/thn,shn->hts/dot_general | solution.py:58
  115.8 6.5 fusion.123
  122.3 7.3 %fusion.124 = f32[128,32,64]{0,2,1:T(8,128)S(1)} fusion(f32[128,32,64]{0,2,1:T(8,128)} %fusion.123, f32[32,64,256]{2,1,0:T(8,128)S(1)} %get-tuple-element.291, f32[512,32,256]{2,0,1:T(8,128)} %get-tuple-element.312, s32[]{:T(128)S(6)} %select_n.102, pred[]{:T(512)S(6)} %compare.7, f32[128,32]{0,1:T(8,128)S(1)} %get-tuple-element.275), kind=kOutput, calls=%fused_computation.23.clone.1 | convolution fusion | flops 806354944 | bytes 8404997 | tf_op jit(solution)/shard_map/while/body/eval_jaxpr/thn,hpn->thp/dot_general | solution.py:61
  129.6 26.4 %dynamic_update_slice.6 = f32[4,128,32,64]{1,0,3,2:T(4,128)} dynamic-update-slice(f32[4,128,32,64]{1,0,3,2:T(4,128)} %get-tuple-element.292, f32[1,128,32,64]{1,0,3,2:T(1,128)S(1)} %bitcast.82, s32[]{:T(128)} %get-tuple-element.290, s32[]{:T(128)} %constant.87.clone.1..sunk.1, s32[]{:T(128)} %constant.87.clone.1..sunk.1, s32[]{:T(128)} %constant.87.clone.1..sunk.1) | dynamic-update-slice | bytes 2097156 | tf_op jit(solution)/shard_map/while/body/jit(dynamic_update_index_in_dim)/dynamic_update_slice | solution.py:149
  156.0 5.7 multiply_add_fusion.4
  163.5 7.9 %fusion.122 = f32[32,128,128]{2,1,0:T(8,128)S(1)} fusion(f32[512,32,256]{2,0,1:T(8,128)} %get-tuple-element.312, s32[]{:T(128)S(6)} %select_n.102, f32[512,32,256]{2,0,1:T(8,128)} %get-tuple-element.311), kind=kOutput, calls=%fused_computation.6.clone.1 | convolution fusion | flops 1610612736 | bytes 10486784 | tf_op jit(solution)/shard_map/while/body/eval_jaxpr/thn,shn->hts/dot_general | solution.py:58
  171.5 6.5 fusion.123
  178.0 7.3 %fusion.124 = f32[128,32,64]{0,2,1:T(8,128)S(1)} fusion(f32[128,32,64]{0,2,1:T(8,128)} %fusion.123, f32[32,64,256]{2,1,0:T(8,128)S(1)} %get-tuple-element.291, f32[512,32,256]{2,0,1:T(8,128)} %get-tuple-element.312, s32[]{:T(128)S(6)} %select_n.102, pred[]{:T(512)S(6)} %compare.7, f32[128,32]{0,1:T(8,128)S(1)} %get-tuple-element.275), kind=kOutput, calls=%fused_computation.23.clone.1 | convolution fusion | flops 806354944 | bytes 8404997 | tf_op jit(solution)/shard_map/while/body/eval_jaxpr/thn,hpn->thp/dot_general | solution.py:61
  185.2 26.4 %dynamic_update_slice.6 = f32[4,128,32,64]{1,0,3,2:T(4,128)} dynamic-update-slice(f32[4,128,32,64]{1,0,3,2:T(4,128)} %get-tuple-element.292, f32[1,128,32,64]{1,0,3,2:T(1,128)S(1)} %bitcast.82, s32[]{:T(128)} %get-tuple-element.290, s32[]{:T(128)} %constant.87.clone.1..sunk.1, s32[]{:T(128)} %constant.87.clone.1..sunk.1, s32[]{:T(128)} %constant.87.clone.1..sunk.1) | dynamic-update-slice | bytes 2097156 | tf_op jit(solution)/shard_map/while/body/jit(dynamic_update_index_in_dim)/dynamic_update_slice | solution.py:149
  211.7 5.7 multiply_add_fusion.4
  219.2 7.9 %fusion.122 = f32[32,128,128]{2,1,0:T(8,128)S(1)} fusion(f32[512,32,256]{2,0,1:T(8,128)} %get-tuple-element.312, s32[]{:T(128)S(6)} %select_n.102, f32[512,32,256]{2,0,1:T(8,128)} %get-tuple-element.311), kind=kOutput, calls=%fused_computation.6.clone.1 | convolution fusion | flops 1610612736 | bytes 10486784 | tf_op jit(solution)/shard_map/while/body/eval_jaxpr/thn,shn->hts/dot_general | solution.py:58
  227.1 6.5 fusion.123
  233.6 7.3 %fusion.124 = f32[128,32,64]{0,2,1:T(8,128)S(1)} fusion(f32[128,32,64]{0,2,1:T(8,128)} %fusion.123, f32[32,64,256]{2,1,0:T(8,128)S(1)} %get-tuple-element.291, f32[512,32,256]{2,0,1:T(8,128)} %get-tuple-element.312, s32[]{:T(128)S(6)} %select_n.102, pred[]{:T(512)S(6)} %compare.7, f32[128,32]{0,1:T(8,128)S(1)} %get-tuple-element.275), kind=kOutput, calls=%fused_computation.23.clone.1 | convolution fusion | flops 806354944 | bytes 8404997 | tf_op jit(solution)/shard_map/while/body/eval_jaxpr/thn,hpn->thp/dot_general | solution.py:61
  240.9 26.4 %dynamic_update_slice.6 = f32[4,128,32,64]{1,0,3,2:T(4,128)} dynamic-update-slice(f32[4,128,32,64]{1,0,3,2:T(4,128)} %get-tuple-element.292, f32[1,128,32,64]{1,0,3,2:T(1,128)S(1)} %bitcast.82, s32[]{:T(128)} %get-tuple-element.290, s32[]{:T(128)} %constant.87.clone.1..sunk.1, s32[]{:T(128)} %constant.87.clone.1..sunk.1, s32[]{:T(128)} %constant.87.clone.1..sunk.1) | dynamic-update-slice | bytes 2097156 | tf_op jit(solution)/shard_map/while/body/jit(dynamic_update_index_in_dim)/dynamic_update_slice | solution.py:149
  267.3 5.7 multiply_add_fusion.4
  273.2 1.1 convert_element_type.73
  275.2 1.2 reduce-window.6
  278.4 5.7 all-reduce
  284.3 5.5 reshape.133
  289.8 19.6 %all-gather.7.cloned.1.call-done = bf16[128,64,256]{2,1,0:T(8,128)(2,1)} async-done(((bf16[32,64,256]{2,1,0:T(8,128)(2,1)}), bf16[128,64,256]{2,1,0:T(8,128)(2,1)}) %all-gather.7.cloned.1.call-update) | async-done | bytes 4194320 | tf_op jit(solution)/shard_map/all_gather | solution.py:26
  309.3 1.6 broadcast_in_dim.39
  310.9 1.0 copy-done.2
  311.9 20.5 %fusion.68 = f32[512,32,64]{0,2,1:T(8,128)} fusion(f32[512,32,64]{0,2,1:T(8,128)} %reshape.133, f32[512,32,64]{0,2,1:T(8,128)} %get-tuple-element.348, f32[512,256]{1,0:T(8,128)S(1)} %copy-done.2, f32[32]{0:T(128)S(1)} %copy-done.6, f32[512,32]{0,1:T(8,128)S(1)} %exponential_bitcast_fusion.1, f32[32,64,256]{2,1,0:T(8,128)} %get-tuple-element.87, ...), kind=kOutput, calls=%fused_computation.70 | convolution fusion | flops 3226468352 | bytes 17367296 | tf_op jit(solution)/shard_map/thn,hpn->thp/dot_general | solution.py:162
  332.4 5.9 copy.36
  338.3 4.8 multiply_reduce_fusion
  343.1 37.3 %psum.7 = f32[8,512]{1,0:T(8,128)S(1)} all-reduce(f32[8,512]{1,0:T(8,128)S(1)} %broadcast_multiply_fusion.1), channel_id=1, replica_groups=mesh['seq'=4,'head'=8] {'head'}, use_global_device_ids=true, to_apply=%region_8.9 | all-reduce | flops 4096 | bytes 32768 | tf_op jit(solution)/shard_map/psum | solution.py:178
  380.5 132.0 %all-gather.5.cloned.1.call-done = bf16[2048,8192]{1,0:T(8,128)(2,1)} async-done(((bf16[2048,2048]{1,0:T(8,128)(2,1)}), bf16[2048,8192]{1,0:T(8,128)(2,1)}) %all-gather.5.cloned.1.call-update) | async-done | bytes 33554448 | tf_op jit(solution)/shard_map/all_gather | solution.py:186
  512.5 28.9 %convolution_convert_fusion = bf16[512,8192]{1,0:T(8,128)(2,1)} fusion(bf16[2048,8192]{1,0:T(8,128)(2,1)} %all-gather.5.cloned.1.call-done, f32[2048]{0:T(1024)S(1)} %copy-done.7, f32[512]{0:T(512)S(1)} %add_rsqrt_fusion, f32[512,2048]{1,0:T(8,128)} %copy.36, bf16[512,2048]{1,0:T(8,128)(2,1)} %param.20), kind=kOutput, calls=%fused_computation.47 | convolution fusion | flops 17193500672 | bytes 48244736 | tf_op jit(solution)/shard_map/dot_general | solution.py:184
  541.6 4.0 add_bitcast_fusion
  545.6 145.0 %reduce-scatter.2.cloned.1.call-done = bf16[64,8192]{1,0:T(8,128)(2,1)} async-done(((bf16[512,8192]{1,0:T(8,128)(2,1)}), bf16[64,8192]{1,0:T(8,128)(2,1)}) %reduce-scatter.2.cloned.1.call-update) | async-done | bytes 1048592 | tf_op jit(solution)/shard_map/reduce_scatter | solution.py:189
  (86 shorter events, 11.2 us)
Async XLA Ops:
  7.2 302.2 %all-gather.7.cloned.1.call-start = ((), (), s32[]{:S(2)}) async-start(), calls=%async_computation.3 | async-start | bytes 5242880 | tf_op jit(solution)/shard_map/all_gather | solution.py:26
  7.2 13.8 %copy-start.3 = (bf16[512,2048]{1,0:T(8,128)(2,1)S(1)}, bf16[512,2048]{1,0:T(8,128)(2,1)}, u32[]{:S(2)}) copy-start(bf16[512,2048]{1,0:T(8,128)(2,1)} %param.19) | copy-start | bytes 6291460
  8.5 15.0 %collective-permute-start.1 = (bf16[3,512]{1,0:T(4,128)(2,1)S(1)}, bf16[3,512]{1,0:T(4,128)(2,1)S(1)}, u32[]{:S(2)}, u32[]{:S(2)}) collective-permute-start(bf16[3,512]{1,0:T(4,128)(2,1)S(1)} %fusion.86), channel_id=1, source_target_pairs={{0,8},{8,16},{16,24},{1,9},{9,17},{17,25},{2,10},{10,18},{18,26},{... | collective-permute-start | bytes 9224 | tf_op jit(solution)/shard_map/ppermute | solution.py:20
  11.6 12.7 %collective-permute-start = (bf16[3,2048]{1,0:T(4,128)(2,1)S(1)}, bf16[3,2048]{1,0:T(4,128)(2,1)S(1)}, u32[]{:S(2)}, u32[]{:S(2)}) collective-permute-start(bf16[3,2048]{1,0:T(4,128)(2,1)S(1)} %slice.68), channel_id=1, source_target_pairs={{0,8},{8,16},{16,24},{1,9},{9,17},{17,25},{2,10},{10,18},{18,26},{... | collective-permute-start | bytes 36872 | tf_op jit(solution)/shard_map/ppermute | solution.py:20
  21.0 3.3 copy-start.4
  21.0 3.3 copy-start.5
  23.5 2.4 copy-start
  24.3 18.6 %copy-start.1 = (f32[512,256]{1,0:T(8,128)}, f32[512,256]{1,0:T(8,128)S(1)}, u32[]{:S(2)}) copy-start(f32[512,256]{1,0:T(8,128)S(1)} %get-tuple-element.155) | copy-start | bytes 1572868
  274.4 2.2 copy-start.8
  274.4 238.1 %all-gather.5.cloned.1.call-start = ((), (), s32[]{:S(2)}) async-start(), calls=%async_computation.1 | async-start | bytes 41943040 | tf_op jit(solution)/shard_map/all_gather | solution.py:186
  275.1 415.5 %reduce-scatter.2.cloned.1.call-start = ((), (), s32[]{:S(2)}) async-start(), calls=%async_computation.2 | async-start | bytes 9437184 | tf_op jit(solution)/shard_map/reduce_scatter | solution.py:189
  310.9 1.0 copy-start.2
  310.9 1.0 copy-start.6
  338.3 174.2 %copy-start.7 = (f32[2048]{0:T(1024)S(1)}, f32[2048]{0:T(1024)}, u32[]{:S(2)}) copy-start(f32[2048]{0:T(1024)} %param.32) | copy-start | bytes 24580
Sparse Core Ops, SparseCore 0:
  274.5 34.7 all-gather.6
  310.9 201.5 all-gather.4
  541.5 149.0 reduce-scatter.1
where the time goes:
time: 701 us; the launch traced here: 697 us
  waiting for transfers between devices  297 us (42%)
  matrix products  159 us (23%)
  local copies, waits for them, and re-layouts  152 us (22%)
  blocking collectives  43 us (6%)
  other arithmetic  21.7 us (3%)
  between operations  14.6 us (2%)
    reduce_scatter x1, waiting for transfers between devices, body(): lax.psum_scatter(terms.astype(jnp.bfloat16), 'head', scatter_dimension=0,...  145 us
    all_gather x1, waiting for transfers between devices, body(): lax.all_gather(out_weight, 'seq', axis=1, tiled=True)  132 us
    dynamic_update_slice x4, local copies, waits for them, and re-layouts, body(): lax.scan(span_step_body, empty_state, jnp.arange(spans_here, dtype=jnp.in...  106 us
    psum x1, blocking collectives, body(): group_totals = lax.psum(contribution, 'head')  37.3 us
    dot_general x4, matrix products, ssd_block(): scores = jnp.einsum('thn,shn->hts', span_c, span_b, precision=highest)  31.5 us
    dot_general x4, matrix products, ssd_block(): carried = jnp.einsum('thn,hpn->thp', span_c, state, precision=highest)  29.1 us
    dot_general x1, matrix products, body(): jnp.dot(normed, lax.all_gather(out_weight, 'seq', axis=1, tiled=True), pr...  28.9 us
    dot_general x4, matrix products, ssd_block(): output = jnp.einsum('hts,shp->thp', mixer, span_x, precision=highest)  26.1 us
  transfers between devices with their start and end apart: 5, of which 3 were waited for; matrix products, arithmetic and copies ran while one was open for 8% of the time, Pallas kernels for 0%

commit v1 on v0

--- a/solution.py
+++ b/solution.py
@@ -12,6 +12,24 @@
 DINNER = 16384
 highest = lax.Precision.HIGHEST
 norm_eps = 1e-05
+
+
+def ring_gather(array, axis, dim):
+    ways, here, lap = (lax.axis_size(axis), lax.axis_index(axis), array.shape[dim])
+    shape = [n * ways if d == dim else n for d, n in enumerate(array.shape)]
+    full = lax.dynamic_update_slice_in_dim(
+        jnp.zeros(shape, array.dtype), array, here * lap, axis=dim
+    )
+    going_up = going_down = array
+    for far in range(1, ways // 2 + 1):
+        going_up = lax.ppermute(going_up, axis, [(d, (d + 1) % ways) for d in range(ways)])
+        full = lax.dynamic_update_slice_in_dim(full, going_up, (here - far) % ways * lap, axis=dim)
+        if 2 * far < ways:
+            going_down = lax.ppermute(going_down, axis, [(d, (d - 1) % ways) for d in range(ways)])
+            full = lax.dynamic_update_slice_in_dim(
+                full, going_down, (here + far) % ways * lap, axis=dim
+            )
+    return full
 
 
 def from_behind(x, axis, by):
@@ -181,11 +199,7 @@
     normed = (
         (pieces * inverse_rms[:, :, None]).reshape(row_count, channels) * norm_gain[None, :]
     ).astype(jnp.bfloat16)
-    terms = jnp.dot(
-        normed,
-        lax.all_gather(out_weight, "seq", axis=1, tiled=True),
-        preferred_element_type=jnp.float32,
-    )
+    terms = jnp.dot(normed, ring_gather(out_weight, "seq", 1), preferred_element_type=jnp.float32)
     layer_out = lax.psum_scatter(
         terms.astype(jnp.bfloat16), "head", scatter_dimension=0, tiled=True
     )

time: 701 us -> 881 us (1.26)
  blocking collectives: 43 us -> 241 us
  waiting for transfers between devices: 297 us -> 149 us
  starting transfers between devices: 6.98 us -> 81.7 us
  local copies, waits for them, and re-layouts: 152 us -> 195 us
    unnamed x1, blocking collectives: 5.73 us -> 204 us
    all_gather x1 -> x0, waiting for transfers between devices: 132 us -> none  [body(): lax.all_gather(out_weight, 'seq', axis=1, tiled=True)]
    ppermute x0 -> x3, starting transfers between devices: none -> 75.2 us  [the longest x2 75.2 us: ring_gather(): lax.ppermute(going_up, axis, [(d, (d + 1) % ways) for d in range(ways)])]
    dynamic_update_slice x0 -> x4, local copies, waits for them, and re-layouts: none -> 33 us  [the longest x2 16.6 us: ring_gather(): lax.dynamic_update_slice_in_dim(full, going_up, (here - far) % ways * lap...]
    all_gather x1, waiting for transfers between devices: 19.6 us -> 0.01 us  [carried_in(): lax.all_gather(a.astype(kind), axis)]
    broadcast_in_dim x0 -> x1, local copies, waits for them, and re-layouts: none -> 10.9 us  [ring_gather(): jnp.zeros(shape, array.dtype)]
  transfers between devices with their start and end apart: 5 -> 7, of which waited for: 3 -> 1; matrix products, arithmetic and copies ran while one was open for 8% -> 39% of each run, Pallas kernels for 0% -> 0%
where the time goes in v1:
time: 881 us; the launch traced here: 873 us
  blocking collectives  241 us (27%)
  local copies, waits for them, and re-layouts  195 us (22%)
  matrix products  165 us (19%)
  waiting for transfers between devices  149 us (17%)
  starting transfers between devices  81.7 us (9%)
  other arithmetic  22.7 us (3%)
  between operations  15.2 us (2%)
    unnamed x1, blocking collectives  204 us
    reduce_scatter x1, waiting for transfers between devices, body(): lax.psum_scatter(terms.astype(jnp.bfloat16), 'head', scatter_dimension=0,...  149 us
    dynamic_update_slice x4, local copies, waits for them, and re-layouts, body(): lax.scan(span_step_body, empty_state, jnp.arange(spans_here, dtype=jnp.in...  106 us
    ppermute x2, starting transfers between devices, ring_gather(): lax.ppermute(going_up, axis, [(d, (d + 1) % ways) for d in range(ways)])  75.2 us
    psum x1, blocking collectives, body(): group_totals = lax.psum(contribution, 'head')  37.7 us
    dot_general x4, matrix products, ssd_block(): scores = jnp.einsum('thn,shn->hts', span_c, span_b, precision=highest)  35.4 us
    dot_general x4, matrix products, ssd_block(): carried = jnp.einsum('thn,hpn->thp', span_c, state, precision=highest)  29.1 us
    dot_general x4, matrix products, ssd_block(): output = jnp.einsum('hts,shp->thp', mixer, span_x, precision=highest)  28.8 us
  transfers between devices with their start and end apart: 7, of which 1 were waited for; matrix products, arithmetic and copies ran while one was open for 39% of the time, Pallas kernels for 0%

profile of v1, /device:TPU:0, one launch (start us, length us, event | category | flops | bytes accessed | tf_op | source)
XLA Modules:
  0.0 872.9 jit_solution(7817580321651426835)
XLA Ops:
  8.5 4.5 collective-permute-start
  13.0 1.1 constant_dynamic-slice_fusion.4
  14.1 1.9 collective-permute-start.1
  21.0 4.0 convert_element_type.65
  25.8 1.5 copy-done
  27.4 4.0 fusion.73
  31.3 5.3 copy.32
  36.7 7.6 reshape.131
  44.3 7.6 reshape.132
  51.9 229.7 %while.26 = (s32[]{:T(128)}, f32[32,64,256]{2,1,0:T(8,128)S(1)}, f32[4,128,32,64]{1,0,3,2:T(4,128)}, s32[4]{0:T(128)S(1)}, f32[32,512]{1,0:T(8,128)S(1)}, /*inde...) while((s32[]{:T(128)}, f32[32,64,256]{2,1,0:T(8,128)S(1)}, ...), condition=%wide.region_2.3_spmd.clone, body=%wide.region_0.2_spmd.clone.sunk | while | flops 3629928448 | bytes 34868712 | solution.py:167
  53.6 8.8 %fusion.122 = f32[32,128,128]{2,1,0:T(8,128)} fusion(f32[512,32,256]{2,0,1:T(8,128)} %get-tuple-element.312, s32[]{:T(128)S(6)} %select_n.135, f32[512,32,256]{2,0,1:T(8,128)} %get-tuple-element.311), kind=kOutput, calls=%fused_computation.6.clone.1 | convolution fusion | flops 1610612736 | bytes 10486784 | tf_op jit(solution)/shard_map/while/body/eval_jaxpr/thn,shn->hts/dot_general | solution.py:76
  63.0 7.2 fusion.123
  70.2 7.3 fusion.124
  77.5 5.7 multiply_add_fusion.4
  83.2 26.4 %dynamic_update_slice.26 = f32[4,128,32,64]{1,0,3,2:T(4,128)} dynamic-update-slice(f32[4,128,32,64]{1,0,3,2:T(4,128)} %get-tuple-element.292, f32[1,128,32,64]{1,0,3,2:T(1,128)S(1)} %bitcast.82, s32[]{:T(128)S(6)} %copy.56, s32[]{:T(128)} %constant.111.clone.1..sunk.1, s32[]{:T(128)} %constant.111.clone.1..sunk.1, s32[]{:T(128)} %constant.111.clone.1..sunk.1) | dynamic-update-slice | bytes 2097156 | tf_op jit(solution)/shard_map/while/body/jit(dynamic_update_index_in_dim)/dynamic_update_slice | solution.py:167
  110.9 8.8 %fusion.122 = f32[32,128,128]{2,1,0:T(8,128)} fusion(f32[512,32,256]{2,0,1:T(8,128)} %get-tuple-element.312, s32[]{:T(128)S(6)} %select_n.135, f32[512,32,256]{2,0,1:T(8,128)} %get-tuple-element.311), kind=kOutput, calls=%fused_computation.6.clone.1 | convolution fusion | flops 1610612736 | bytes 10486784 | tf_op jit(solution)/shard_map/while/body/eval_jaxpr/thn,shn->hts/dot_general | solution.py:76
  120.3 7.2 fusion.123
  127.5 7.3 fusion.124
  134.8 5.7 multiply_add_fusion.4
  140.5 26.4 %dynamic_update_slice.26 = f32[4,128,32,64]{1,0,3,2:T(4,128)} dynamic-update-slice(f32[4,128,32,64]{1,0,3,2:T(4,128)} %get-tuple-element.292, f32[1,128,32,64]{1,0,3,2:T(1,128)S(1)} %bitcast.82, s32[]{:T(128)S(6)} %copy.56, s32[]{:T(128)} %constant.111.clone.1..sunk.1, s32[]{:T(128)} %constant.111.clone.1..sunk.1, s32[]{:T(128)} %constant.111.clone.1..sunk.1) | dynamic-update-slice | bytes 2097156 | tf_op jit(solution)/shard_map/while/body/jit(dynamic_update_index_in_dim)/dynamic_update_slice | solution.py:167
  168.1 8.8 %fusion.122 = f32[32,128,128]{2,1,0:T(8,128)} fusion(f32[512,32,256]{2,0,1:T(8,128)} %get-tuple-element.312, s32[]{:T(128)S(6)} %select_n.135, f32[512,32,256]{2,0,1:T(8,128)} %get-tuple-element.311), kind=kOutput, calls=%fused_computation.6.clone.1 | convolution fusion | flops 1610612736 | bytes 10486784 | tf_op jit(solution)/shard_map/while/body/eval_jaxpr/thn,shn->hts/dot_general | solution.py:76
  177.6 7.2 fusion.123
  184.8 7.3 fusion.124
  192.1 5.7 multiply_add_fusion.4
  197.8 26.4 %dynamic_update_slice.26 = f32[4,128,32,64]{1,0,3,2:T(4,128)} dynamic-update-slice(f32[4,128,32,64]{1,0,3,2:T(4,128)} %get-tuple-element.292, f32[1,128,32,64]{1,0,3,2:T(1,128)S(1)} %bitcast.82, s32[]{:T(128)S(6)} %copy.56, s32[]{:T(128)} %constant.111.clone.1..sunk.1, s32[]{:T(128)} %constant.111.clone.1..sunk.1, s32[]{:T(128)} %constant.111.clone.1..sunk.1) | dynamic-update-slice | bytes 2097156 | tf_op jit(solution)/shard_map/while/body/jit(dynamic_update_index_in_dim)/dynamic_update_slice | solution.py:167
  225.4 8.8 %fusion.122 = f32[32,128,128]{2,1,0:T(8,128)} fusion(f32[512,32,256]{2,0,1:T(8,128)} %get-tuple-element.312, s32[]{:T(128)S(6)} %select_n.135, f32[512,32,256]{2,0,1:T(8,128)} %get-tuple-element.311), kind=kOutput, calls=%fused_computation.6.clone.1 | convolution fusion | flops 1610612736 | bytes 10486784 | tf_op jit(solution)/shard_map/while/body/eval_jaxpr/thn,shn->hts/dot_general | solution.py:76
  234.8 7.2 fusion.123
  242.1 7.3 fusion.124
  249.3 5.7 multiply_add_fusion.4
  255.0 26.4 %dynamic_update_slice.26 = f32[4,128,32,64]{1,0,3,2:T(4,128)} dynamic-update-slice(f32[4,128,32,64]{1,0,3,2:T(4,128)} %get-tuple-element.292, f32[1,128,32,64]{1,0,3,2:T(1,128)S(1)} %bitcast.82, s32[]{:T(128)S(6)} %copy.56, s32[]{:T(128)} %constant.111.clone.1..sunk.1, s32[]{:T(128)} %constant.111.clone.1..sunk.1, s32[]{:T(128)} %constant.111.clone.1..sunk.1) | dynamic-update-slice | bytes 2097156 | tf_op jit(solution)/shard_map/while/body/jit(dynamic_update_index_in_dim)/dynamic_update_slice | solution.py:167
  281.6 1.1 convert_element_type.73
  282.9 74.7 %collective-permute-start.4 = (bf16[2048,2048]{1,0:T(8,128)(2,1)}, bf16[2048,2048]{1,0:T(8,128)(2,1)}, u32[]{:S(2)}, u32[]{:S(2)}) collective-permute-start(bf16[2048,2048]{1,0:T(8,128)(2,1)} %collective-permute-done.2), channel_id=1, source_target_pairs={{0,8},{8,16},{16,24},{24,0},{1,9},{9,17},{17,25},{25,1},{2,10},{10... | collective-permute-start | bytes 25165832 | tf_op jit(solution)/shard_map/ppermute | solution.py:25
  357.6 1.2 reduce-window.6
  360.7 203.7 %all-reduce = bf16[128]{0:T(256)(128)(2,1)S(1)} all-reduce(bf16[128]{0:T(256)(128)(2,1)S(1)} %dynamic-update-slice), channel_id=2, replica_groups=mesh['seq'=4,'head'=8] {'seq'}, use_global_device_ids=true, to_apply=%add | all-reduce | flops 128 | bytes 512
  564.6 10.9 %broadcast_in_dim.44 = bf16[2048,8192]{1,0:T(8,128)(2,1)} broadcast(bf16[]{:T(256)} %constant.132.clone.1), dimensions={} | broadcast | bytes 33554432 | tf_op jit(solution)/shard_map/broadcast_in_dim | solution.py:21
  575.5 8.2 constant_dynamic-update-slice_fusion.3
  583.8 5.5 reshape.133
  589.2 1.6 broadcast_in_dim.41
  591.8 20.5 %fusion.68 = f32[512,32,64]{0,2,1:T(8,128)} fusion(f32[512,32,64]{0,2,1:T(8,128)} %reshape.133, f32[512,32,64]{0,2,1:T(8,128)} %get-tuple-element.347, f32[512,256]{1,0:T(8,128)S(1)} %copy-done.3, f32[32]{0:T(128)S(1)} %copy-done.6, f32[512,32]{0,1:T(8,128)S(1)} %exponential_bitcast_fusion.1, f32[32,64,256]{2,1,0:T(8,128)} %get-tuple-element.87, ...), kind=kOutput, calls=%fused_computation.70 | convolution fusion | flops 3226468352 | bytes 17367296 | tf_op jit(solution)/shard_map/thn,hpn->thp/dot_general | solution.py:180
  612.3 5.4 copy.36
  617.7 4.2 multiply_reduce_fusion
  622.0 37.7 %psum.7 = f32[8,512]{1,0:T(8,128)S(1)} all-reduce(f32[8,512]{1,0:T(8,128)S(1)} %broadcast_multiply_fusion.1), channel_id=1, replica_groups=mesh['seq'=4,'head'=8] {'head'}, use_global_device_ids=true, to_apply=%region_8.9 | all-reduce | flops 4096 | bytes 32768 | tf_op jit(solution)/shard_map/psum | solution.py:196
  659.9 8.2 constant_dynamic-update-slice_fusion.2
  668.1 8.2 constant_dynamic-update-slice_fusion.1
  676.3 8.4 constant_dynamic-update-slice_fusion
  684.7 27.9 %convolution_convert_fusion = bf16[512,8192]{1,0:T(8,128)(2,1)} fusion(bf16[2048,8192]{1,0:T(8,128)(2,1)} %constant_dynamic-update-slice_fusion, f32[2048]{0:T(1024)S(1)} %copy-done.7, f32[512]{0:T(512)S(1)} %add_rsqrt_fusion, f32[512,2048]{1,0:T(8,128)S(1)} %copy-done.1, bf16[512,2048]{1,0:T(8,128)(2,1)} %param.20), kind=kOutput, calls=%fused_computation.47 | convolution fusion | flops 17193500672 | bytes 48244736 | tf_op jit(solution)/shard_map/dot_general | solution.py:202
  712.8 4.0 add_bitcast_fusion
  716.7 149.1 %reduce-scatter.2.cloned.1.call-done = bf16[64,8192]{1,0:T(8,128)(2,1)} async-done(((bf16[512,8192]{1,0:T(8,128)(2,1)}), bf16[64,8192]{1,0:T(8,128)(2,1)}) %reduce-scatter.2.cloned.1.call-update) | async-done | bytes 1048592 | tf_op jit(solution)/shard_map/reduce_scatter | solution.py:203
  (94 shorter events, 14.7 us)
Async XLA Ops:
  7.2 582.1 %all-gather.4.cloned.1.call-start = ((), (), s32[]{:S(2)}) async-start(), calls=%async_computation.2 | async-start | bytes 5242880 | tf_op jit(solution)/shard_map/all_gather | solution.py:44
  7.2 275.7 %collective-permute-start.2 = (bf16[2048,2048]{1,0:T(8,128)(2,1)}, bf16[2048,2048]{1,0:T(8,128)(2,1)}, u32[]{:S(2)}, u32[]{:S(2)}) collective-permute-start(bf16[2048,2048]{1,0:T(8,128)(2,1)} %param.33), channel_id=1, source_target_pairs={{0,8},{8,16},{16,24},{24,0},{1,9},{9,17},{17,25},{25,1},{2,10},{10... | collective-permute-start | bytes 25165832 | tf_op jit(solution)/shard_map/ppermute | solution.py:25
  8.5 17.3 %collective-permute-start = (bf16[3,2048]{1,0:T(4,128)(2,1)S(1)}, bf16[3,2048]{1,0:T(4,128)(2,1)S(1)}, u32[]{:S(2)}, u32[]{:S(2)}) collective-permute-start(bf16[3,2048]{1,0:T(4,128)(2,1)S(1)} %slice.68), channel_id=1, source_target_pairs={{0,8},{8,16},{16,24},{1,9},{9,17},{17,25},{2,10},{10,18},{18,26},{... | collective-permute-start | bytes 36872 | tf_op jit(solution)/shard_map/ppermute | solution.py:38
  14.1 10.9 %collective-permute-start.1 = (bf16[3,512]{1,0:T(4,128)(2,1)S(1)}, bf16[3,512]{1,0:T(4,128)(2,1)S(1)}, u32[]{:S(2)}, u32[]{:S(2)}) collective-permute-start(bf16[3,512]{1,0:T(4,128)(2,1)S(1)} %fusion.86), channel_id=1, source_target_pairs={{0,8},{8,16},{16,24},{1,9},{9,17},{17,25},{2,10},{10,18},{18,26},{... | collective-permute-start | bytes 9224 | tf_op jit(solution)/shard_map/ppermute | solution.py:38
  20.9 4.9 copy-start.4
  21.0 4.9 copy-start.5
  25.0 2.4 copy-start
  25.8 18.5 %copy-start.2 = (f32[512,256]{1,0:T(8,128)}, f32[512,256]{1,0:T(8,128)S(1)}, u32[]{:S(2)}) copy-start(f32[512,256]{1,0:T(8,128)S(1)} %get-tuple-element.155) | copy-start | bytes 1572868
  281.6 77.3 %copy-start.8 = (u32[32]{0:T(128)S(1)}, u32[32]{0:T(128)}, u32[]{:S(2)}) copy-start(u32[32]{0:T(128)} %constant.139) | copy-start | bytes 388
  282.8 583.0 %reduce-scatter.2.cloned.1.call-start = ((), (), s32[]{:S(2)}) async-start(), calls=%async_computation.1 | async-start | bytes 9437184 | tf_op jit(solution)/shard_map/reduce_scatter | solution.py:203
  282.8 385.3 %collective-permute-start.3 = (bf16[2048,2048]{1,0:T(8,128)(2,1)}, bf16[2048,2048]{1,0:T(8,128)(2,1)}, u32[]{:S(2)}, u32[]{:S(2)}) collective-permute-start(bf16[2048,2048]{1,0:T(8,128)(2,1)} %param.33), channel_id=1, source_target_pairs={{0,24},{8,0},{16,8},{24,16},{1,25},{9,1},{17,9},{25,17},{2,26},{10... | collective-permute-start | bytes 25165832 | tf_op jit(solution)/shard_map/ppermute | solution.py:28
  282.9 393.4 %collective-permute-start.4 = (bf16[2048,2048]{1,0:T(8,128)(2,1)}, bf16[2048,2048]{1,0:T(8,128)(2,1)}, u32[]{:S(2)}, u32[]{:S(2)}) collective-permute-start(bf16[2048,2048]{1,0:T(8,128)(2,1)} %collective-permute-done.2), channel_id=1, source_target_pairs={{0,8},{8,16},{16,24},{24,0},{1,9},{9,17},{17,25},{25,1},{2,10},{10... | collective-permute-start | bytes 25165832 | tf_op jit(solution)/shard_map/ppermute | solution.py:25
  590.8 1.0 copy-start.3
  590.8 1.0 copy-start.6
  676.3 8.4 copy-start.1
  676.3 8.4 copy-start.7
Sparse Core Ops, SparseCore 0:
  282.9 133.7 all-gather.3
  712.7 153.0 reduce-scatter.1
